TPU v7x, 128 devices: a whole 4x4x4 slice. The times are simulated.
128 devices in a mesh: rows: 16 (over z, x), cols: 8 (over y, core).
Axes of the slice: x: 4, y: 4, z: 4, core: 2. Of those that a mesh axis runs over, the one named last changes fastest.
Arguments:
- trailing: bfloat16 [32, 16, 1024, 1024], P('rows', 'cols'), may hold values from -6 to 6
- row_left: bfloat16 [3, 32, 1024, 384], P(None, 'rows', 'cols'), may hold values from -0.5 to 0.5
- row_right: bfloat16 [3, 32, 1024, 384], P(None, 'rows', 'cols'), may hold values from -0.5 to 0.5
- column_left: bfloat16 [3, 16, 1024, 384], P(None, 'cols', 'rows'), may hold values from -0.5 to 0.5
- column_right: bfloat16 [3, 16, 1024, 384], P(None, 'cols', 'rows'), may hold values from -0.5 to 0.5
- row_ranks: int32 [3, 32], replicated, may hold values from 64 to 384, as said below
- column_ranks: int32 [3, 16], P(None, 'cols'), may hold values from 64 to 384, as said below
Outputs:
- updated: float32 [32, 16, 1024, 1024], P('rows', 'cols')
Inputs may be any that keep to these rules, and one draw needn't show every extreme that they name: `row_ranks`: every rank is a multiple of 64. `column_ranks`: every rank is a multiple of 64.
All inputs are finite; a program needn't handle non-finite values.
Results may differ from a plain program's by a relative error of at most 0.0026.
Values may be sent and summed in bfloat16 or wider, within the bound.
A program may use at most 128 MiB of HBM per device.

v0:
```python
import jax
import jax.numpy as jnp
from jax import lax
from jax.sharding import PartitionSpec as P


def on_device(trailing, row_left, row_right, column_left, column_right, row_ranks, column_ranks):
    rows_here = trailing.shape[0]
    panels = row_left.shape[0]
    width = row_left.shape[3]
    here = lax.axis_index("rows")
    own_ranks = lax.dynamic_slice_in_dim(row_ranks, here * rows_here, rows_here, 1)
    keep_mask = (
        jnp.arange(width, dtype=jnp.int32)[None, None, :] < column_ranks[:, :, None]
    ).astype(jnp.bfloat16)
    row_mask = (jnp.arange(width, dtype=jnp.int32)[None, None, :] < own_ranks[:, :, None]).astype(
        jnp.bfloat16
    )
    full_left, full_right = (
        lax.all_gather(row_left, "cols", axis=2, tiled=True),
        lax.all_gather(row_right, "cols", axis=2, tiled=True),
    )
    gathered_left, gathered_right = (
        lax.all_gather(column_left, "rows", axis=2, tiled=True),
        lax.all_gather(column_right, "rows", axis=2, tiled=True),
    )
    column_sets = []
    for panel in range(panels):
        column_sets.append(
            (
                gathered_left[panel] * keep_mask[panel][:, None, :],
                gathered_right[panel] * keep_mask[panel][:, None, :],
            )
        )
    results = []
    for row_pos in range(rows_here):
        lefts = []
        rights = []
        for panel in range(panels):
            mask_here = row_mask[panel, row_pos][None, :]
            left_tile = full_left[panel, row_pos] * mask_here
            right_tile = full_right[panel, row_pos] * mask_here
            core = jnp.einsum(
                "bk,jbr->jkr", right_tile, column_sets[panel][1], preferred_element_type=jnp.float32
            ).astype(jnp.bfloat16)
            projected = jnp.einsum(
                "jkr,jcr->jkc", core, column_sets[panel][0], preferred_element_type=jnp.float32
            ).astype(jnp.bfloat16)
            lefts.append(left_tile)
            rights.append(projected)
        left_all = jnp.concatenate(lefts, axis=1)
        right_all = jnp.concatenate(rights, axis=1)
        results.append(
            jnp.einsum("bk,jkc->jbc", left_all, right_all, preferred_element_type=jnp.float32)
        )
    update = jnp.stack(results)
    return trailing.astype(jnp.float32) - update


def solution(mesh):
    return jax.shard_map(
        on_device,
        mesh=mesh,
        in_specs=(
            P("rows", "cols", None, None),
            P(None, "rows", "cols", None),
            P(None, "rows", "cols", None),
            P(None, "cols", "rows", None),
            P(None, "cols", "rows", None),
            P(),
            P(None, "cols"),
        ),
        out_specs=P("rows", "cols", None, None),
        check_vma=False,
    )
```

profile of v0, /device:TPU:1, one launch (start us, length us, event | category | flops | bytes accessed | tf_op | source)
XLA Modules:
  0.0 279.5 jit_solution(346697571027519142)
XLA Ops:
  6.5 0.0 copy-start
  6.5 0.0 all-gather.11.cloned.1.call-start
  6.5 0.7 all-gather.11.cloned.1.call-update
  7.3 0.0 all-gather.7.cloned.1.call-start
  7.3 0.7 all-gather.7.cloned.1.call-update
  8.0 0.0 all-gather.9.cloned.1.call-start
  8.1 0.7 all-gather.9.cloned.1.call-update
  8.7 0.0 all-gather.5.cloned.1.call-start
  8.8 0.5 all-gather.5.cloned.1.call-update
  9.3 0.8 copy.9
  10.1 11.4 %copy.8 = bf16[2,2,1024,1024]{2,3,1,0:T(8,128)(2,1)} copy(bf16[2,2,1024,1024]{3,2,1,0:T(8,128)(2,1)} %param.7) | data formatting | bytes 16777216 | tf_op args[0]
  21.5 0.0 copy-done
  21.5 0.1 constant_dynamic-slice_fusion
  21.5 0.1 compare_convert_fusion
  21.6 0.1 compare_convert_fusion.1
  21.7 25.3 %all-gather.11.cloned.1.call-done = bf16[3,2,1024,384]{3,2,1,0:T(8,128)(2,1)} async-done(((bf16[3,2,128,384]{3,2,1,0:T(8,128)(2,1)}), bf16[3,2,1024,384]{3,2,1,0:T(8,128)(2,1)}) %all-gather.11.cloned.1.call-update) | async-done | bytes 4718608 | tf_op jit(solution)/shard_map/all_gather | solution.py:20
  47.0 3.9 %fusion.55 = (bf16[1024,384]{1,0:T(8,128)(2,1)S(1)}, bf16[1024,384]{1,0:T(8,128)(2,1)S(1)}, bf16[1024,384]{1,0:T(8,128)(2,1)S(1)}, bf16[1024,384]{1,0:T(8,128)(2...) fusion(bf16[3,2,1024,384]{3,2,1,0:T(8,128)(2,1)} %all-gather.11.cloned.1.call-done, ...), kind=kLoop, calls=%fused_computation.66 | loop fusion | flops 2359296 | bytes 9441792 | tf_op jit(solution)/shard_map/mul | solution.py:41
  51.0 32.1 %all-gather.7.cloned.1.call-done = bf16[3,2,1024,384]{3,2,1,0:T(8,128)(2,1)} async-done(((bf16[3,2,128,384]{3,2,1,0:T(8,128)(2,1)}), bf16[3,2,1024,384]{3,2,1,0:T(8,128)(2,1)}) %all-gather.7.cloned.1.call-update) | async-done | bytes 4718608 | tf_op jit(solution)/shard_map/all_gather | solution.py:21
  83.1 55.8 %all-gather.9.cloned.1.call-done = bf16[3,2,1024,384]{3,2,1,0:T(8,128)(2,1)} async-done(((bf16[3,2,64,384]{3,2,1,0:T(8,128)(2,1)}), bf16[3,2,1024,384]{3,2,1,0:T(8,128)(2,1)}) %all-gather.9.cloned.1.call-update) | async-done | bytes 4718608 | tf_op jit(solution)/shard_map/all_gather | solution.py:24
  138.9 55.7 %all-gather.5.cloned.1.call-done = bf16[3,2,1024,384]{3,2,1,0:T(8,128)(2,1)} async-done(((bf16[3,2,64,384]{3,2,1,0:T(8,128)(2,1)}), bf16[3,2,1024,384]{3,2,1,0:T(8,128)(2,1)}) %all-gather.5.cloned.1.call-update) | async-done | bytes 4718608 | tf_op jit(solution)/shard_map/all_gather | solution.py:25
  194.6 5.3 %convolution_convert_fusion.4 = bf16[2,384,1024]{1,2,0:T(8,128)(2,1)} fusion(bf16[3,2,1024,384]{3,2,1,0:T(8,128)(2,1)} %all-gather.9.cloned.1.call-done, bf16[2,384]{1,0:T(2,128)(2,1)S(1)} %get-tuple-element.19, bf16[3,2,1024,384]{3,2,1,0:T(8,128)(2,1)} %all-gather.5.cloned.1.call-done, bf16[3,2,1024,384]{3,2,1,0:T(8,128)(2,1)} %all-gather.7.cloned.1.call-done, ...), kind=kOutput, calls=%fused_computation.29 | convolution fusion | flops 1213366272 | bytes 5509120 | tf_op jit(solution)/shard_map/jkr,jcr->jkc/dot_general | solution.py:46
  199.9 5.3 %convolution_convert_fusion.3 = bf16[2,384,1024]{1,2,0:T(8,128)(2,1)} fusion(bf16[3,2,1024,384]{3,2,1,0:T(8,128)(2,1)} %all-gather.9.cloned.1.call-done, bf16[2,384]{1,0:T(2,128)(2,1)S(1)} %get-tuple-element.18, bf16[3,2,1024,384]{3,2,1,0:T(8,128)(2,1)} %all-gather.5.cloned.1.call-done, bf16[3,2,1024,384]{3,2,1,0:T(8,128)(2,1)} %all-gather.7.cloned.1.call-done, ...), kind=kOutput, calls=%fused_computation.28 | convolution fusion | flops 1213366272 | bytes 5509120 | tf_op jit(solution)/shard_map/jkr,jcr->jkc/dot_general | solution.py:46
  205.2 5.3 %convolution_convert_fusion.5 = bf16[2,384,1024]{1,2,0:T(8,128)(2,1)} fusion(bf16[3,2,1024,384]{3,2,1,0:T(8,128)(2,1)} %all-gather.9.cloned.1.call-done, bf16[2,384]{1,0:T(2,128)(2,1)S(1)} %get-tuple-element.17, bf16[3,2,1024,384]{3,2,1,0:T(8,128)(2,1)} %all-gather.5.cloned.1.call-done, bf16[3,2,1024,384]{3,2,1,0:T(8,128)(2,1)} %all-gather.7.cloned.1.call-done, ...), kind=kOutput, calls=%fused_computation.30 | convolution fusion | flops 1213366272 | bytes 5509120 | tf_op jit(solution)/shard_map/jkr,jcr->jkc/dot_general | solution.py:46
  210.4 9.9 %fusion.15 = f32[1,2,1024,1024]{2,3,1,0:T(8,128)} fusion(bf16[2,384,1024]{1,2,0:T(8,128)(2,1)} %convolution_convert_fusion.3, bf16[2,384,1024]{1,2,0:T(8,128)(2,1)} %convolution_convert_fusion.4, bf16[2,384,1024]{1,2,0:T(8,128)(2,1)} %convolution_convert_fusion.5, bf16[1024,384]{1,0:T(8,128)(2,1)} %get-tuple-element.15, ...), kind=kOutput, calls=%fused_computation.14 | convolution fusion | flops 4853071872 | bytes 15466496 | tf_op jit(solution)/shard_map/bk,jkc->jbc/dot_general | solution.py:54
  220.4 5.3 %convolution_convert_fusion.1 = bf16[2,384,1024]{1,2,0:T(8,128)(2,1)} fusion(bf16[3,2,1024,384]{3,2,1,0:T(8,128)(2,1)} %all-gather.9.cloned.1.call-done, bf16[2,384]{1,0:T(2,128)(2,1)S(1)} %get-tuple-element.19, bf16[3,2,1024,384]{3,2,1,0:T(8,128)(2,1)} %all-gather.5.cloned.1.call-done, bf16[3,2,1024,384]{3,2,1,0:T(8,128)(2,1)} %all-gather.7.cloned.1.call-done, ...), kind=kOutput, calls=%fused_computation.26 | convolution fusion | flops 1213366272 | bytes 5509120 | tf_op jit(solution)/shard_map/jkr,jcr->jkc/dot_general | solution.py:46
  225.7 5.3 %convolution_convert_fusion = bf16[2,384,1024]{1,2,0:T(8,128)(2,1)} fusion(bf16[3,2,1024,384]{3,2,1,0:T(8,128)(2,1)} %all-gather.9.cloned.1.call-done, bf16[2,384]{1,0:T(2,128)(2,1)S(1)} %get-tuple-element.18, bf16[3,2,1024,384]{3,2,1,0:T(8,128)(2,1)} %all-gather.5.cloned.1.call-done, bf16[3,2,1024,384]{3,2,1,0:T(8,128)(2,1)} %all-gather.7.cloned.1.call-done, ...), kind=kOutput, calls=%fused_computation.25 | convolution fusion | flops 1213366272 | bytes 5509120 | tf_op jit(solution)/shard_map/jkr,jcr->jkc/dot_general | solution.py:46
  230.9 5.3 %convolution_convert_fusion.2 = bf16[2,384,1024]{1,2,0:T(8,128)(2,1)} fusion(bf16[3,2,1024,384]{3,2,1,0:T(8,128)(2,1)} %all-gather.9.cloned.1.call-done, bf16[2,384]{1,0:T(2,128)(2,1)S(1)} %get-tuple-element.17, bf16[3,2,1024,384]{3,2,1,0:T(8,128)(2,1)} %all-gather.5.cloned.1.call-done, bf16[3,2,1024,384]{3,2,1,0:T(8,128)(2,1)} %all-gather.7.cloned.1.call-done, ...), kind=kOutput, calls=%fused_computation.27 | convolution fusion | flops 1213366272 | bytes 5509120 | tf_op jit(solution)/shard_map/jkr,jcr->jkc/dot_general | solution.py:46
  236.2 7.4 %fusion.12 = f32[1,2,1024,1024]{2,3,1,0:T(8,128)S(1)} fusion(bf16[2,384,1024]{1,2,0:T(8,128)(2,1)} %convolution_convert_fusion, bf16[2,384,1024]{1,2,0:T(8,128)(2,1)} %convolution_convert_fusion.1, bf16[2,384,1024]{1,2,0:T(8,128)(2,1)} %convolution_convert_fusion.2, bf16[1024,384]{1,0:T(8,128)(2,1)S(1)} %get-tuple-element.12, ...), kind=kOutput, calls=%fused_computation.13 | convolution fusion | flops 4853071872 | bytes 15466496 | tf_op jit(solution)/shard_map/bk,jkc->jbc/dot_general | solution.py:54
  243.7 12.9 %maximum_subtract_fusion = f32[2,2,1024,1024]{2,3,1,0:T(8,128)} fusion(f32[1,2,1024,1024]{2,3,1,0:T(8,128)S(1)} %fusion.12, f32[1,2,1024,1024]{2,3,1,0:T(8,128)} %fusion.15, bf16[2,2,1024,1024]{2,3,1,0:T(8,128)(2,1)} %copy.8), kind=kLoop, calls=%fused_computation | loop fusion | flops 12582912 | bytes 41943040 | tf_op jit(solution)/shard_map/sub | solution.py:57
  256.5 0.0 copy-start.1
  256.5 16.4 %copy.10 = f32[2,2,1024,1024]{3,2,1,0:T(8,128)} copy(f32[2,2,1024,1024]{2,3,1,0:T(8,128)} %maximum_subtract_fusion) | data formatting | bytes 33554432 | tf_op jit(solution)/shard_map/sub | solution.py:57
  272.9 0.0 copy-done.1
  (2 shorter events, 0.1 us)
Async XLA Ops:
  6.5 14.9 %copy-start = (s32[3,32]{1,0:T(4,128)S(1)}, s32[3,32]{1,0:T(4,128)}, u32[]{:S(2)}) copy-start(s32[3,32]{1,0:T(4,128)} %param.12) | copy-start | bytes 1156
  6.5 40.5 %all-gather.11.cloned.1.call-start = ((), (), s32[]{:S(2)}) async-start(), calls=%async_computation.3 | async-start | bytes 5308416 | tf_op jit(solution)/shard_map/all_gather | solution.py:20
  7.3 75.8 %all-gather.7.cloned.1.call-start = ((), (), s32[]{:S(2)}) async-start(), calls=%async_computation.1 | async-start | bytes 5308416 | tf_op jit(solution)/shard_map/all_gather | solution.py:21
  8.0 130.9 %all-gather.9.cloned.1.call-start = ((), (), s32[]{:S(2)}) async-start(), calls=%async_computation.2 | async-start | bytes 5013504 | tf_op jit(solution)/shard_map/all_gather | solution.py:24
  8.7 185.9 %all-gather.5.cloned.1.call-start = ((), (), s32[]{:S(2)}) async-start(), calls=%async_computation | async-start | bytes 5013504 | tf_op jit(solution)/shard_map/all_gather | solution.py:25
  256.5 16.4 %copy-start.1 = (s32[3,32]{1,0:T(4,128)S(1)}, s32[3,32]{1,0:T(4,128)}, u32[]{:S(2)}) copy-start(s32[3,32]{1,0:T(4,128)} %param.12) | copy-start | bytes 1156
Sparse Core Ops, SparseCore 0:
  9.0 37.9 all-gather.10
  48.7 34.2 all-gather.6
  85.2 53.6 all-gather.8
  140.9 53.6 all-gather.4
where the time goes:
time: 280 us; the launch traced here: 279 us
  waiting for transfers between devices  172 us (61%)
  matrix products  49 us (18%)
  local copies, waits for them, and re-layouts  28.7 us (10%)
  other arithmetic  16.9 us (6%)
  between operations  13.2 us (5%)
    all_gather x1, waiting for transfers between devices, on_device(): lax.all_gather(column_left, 'rows', axis=2, tiled=True)  55.8 us
    all_gather x1, waiting for transfers between devices, on_device(): lax.all_gather(column_right, 'rows', axis=2, tiled=True)  55.7 us
    all_gather x1, waiting for transfers between devices, on_device(): lax.all_gather(row_right, 'cols', axis=2, tiled=True)  32.1 us
    dot_general x6, matrix products, on_device(): jnp.einsum('jkr,jcr->jkc', core, column_sets[panel][0], preferred_element...  31.7 us
    all_gather x1, waiting for transfers between devices, on_device(): lax.all_gather(row_left, 'cols', axis=2, tiled=True)  25.3 us
    dot_general x2, matrix products, on_device(): jnp.einsum('bk,jkc->jbc', left_all, right_all, preferred_element_type=jnp...  17.4 us
    sub x1, local copies, waits for them, and re-layouts, on_device(): return trailing.astype(jnp.float32) - update  16.4 us
    sub x1, other arithmetic, on_device(): return trailing.astype(jnp.float32) - update  12.9 us
  transfers between devices with their start and end apart: 4, of which 4 were waited for; matrix products, arithmetic and copies ran while one was open for 6% of the time, Pallas kernels for 0%

commit v1 on v0

v1 whole, which is shorter than its diff:
```python
import jax
import jax.numpy as jnp
from jax import lax
from jax.experimental import pallas as pl
from jax.experimental.pallas import tpu as pltpu
from jax.sharding import PartitionSpec as P

SIDE = 4
MESH = pl.DeviceIdType.MESH


class Grid:
    def __init__(self):
        self.r = lax.axis_index("rows")
        self.c = lax.axis_index("cols")
        self.z, self.x = self.r // SIDE, self.r % SIDE
        self.y, self.core = self.c // 2, self.c % 2

    def shifted(self, axis, step):
        return (getattr(self, axis) + (step + SIDE)) % SIDE

    def neighbour(self, axis, step):
        if axis == "z":
            return (self.shifted("z", step) * SIDE + self.x, self.c)
        if axis == "x":
            return (self.z * SIDE + self.shifted("x", step), self.c)
        if axis == "y":
            return (self.r, self.shifted("y", step) * 2 + self.core)
        return (self.r, self.y * 2 + (1 - self.core))


class Messages:
    def __init__(self, send_sem, recv_sem):
        self.send_sem, self.recv_sem = send_sem, recv_sem
        self.sent = {}

    def send(self, key, view, target):
        index = len(self.sent)
        copy = pltpu.make_async_remote_copy(
            src_ref=view,
            dst_ref=view,
            send_sem=self.send_sem.at[index],
            recv_sem=self.recv_sem.at[index],
            device_id=target,
            device_id_type=MESH,
        )
        copy.start()
        self.sent[key] = copy

    def got(self, key):
        self.sent[key].wait_recv()

    def drain(self):
        for copy in self.sent.values():
            copy.wait_send()


class ColumnStream:
    def __init__(self, name, grid, messages, buf, first, second):
        self.name, self.grid, self.messages, self.buf = name, grid, messages, buf
        self.a, self.b = first, second

    def view(self, da, db, half=None):
        place = {self.a: self.grid.shifted(self.a, da), self.b: self.grid.shifted(self.b, db)}
        if half is None:
            return self.buf.at[:, place["z"], place["x"]]
        part = self.buf.shape[3] // 2
        return self.buf.at[:, place["z"], place["x"], pl.ds(half * part, part)]

    def send(self, kind, da, db, axis, step, half=None):
        self.messages.send(
            (self.name, kind, da, step), self.view(da, db, half), self.grid.neighbour(axis, step)
        )

    def got(self, kind, da, step):
        self.messages.got((self.name, kind, da, step))

    def start_a(self):
        for step in (1, -1):
            self.send("a", 0, 0, self.a, step)

    def start_b(self):
        for step in (1, -1):
            self.send("b", 0, 0, self.b, step)

    def e1(self):
        for step in (1, -1):
            self.got("a", 0, step)
            self.messages.send(
                (self.name, "ah", 0, step),
                self.view(-step, 0, 0 if step == 1 else 1),
                self.grid.neighbour(self.a, step),
            )
            for out in (1, -1):
                self.send("b", -step, 0, self.b, out)

    def relay(self, da):
        for step in (1, -1):
            self.got("b", da, step)
            self.send("bh", da, -step, self.b, step, 0 if step == 1 else 1)

    def e2(self):
        self.relay(0)

    def e3(self):
        for step in (1, -1):
            self.got("ah", 0, step)
        for out in (1, -1):
            self.send("b", 2, 0, self.b, out)

    def e4(self):
        self.relay(1)
        self.relay(-1)

    def e5(self):
        self.relay(2)

    def e6(self):
        for da in (0, 1, -1, 2):
            for step in (1, -1):
                self.got("bh", da, step)


class RowStream:
    def __init__(self, name, grid, messages, buf):
        self.name, self.grid, self.messages, self.buf = name, grid, messages, buf

    def view(self, dy, half=None):
        place = self.grid.shifted("y", dy) * 2 + self.grid.core
        if half is None:
            return self.buf.at[:, place]
        part = self.buf.shape[2] // 2
        return self.buf.at[:, place, pl.ds(half * part, part)]

    def share(self, dy):
        self.messages.send((self.name, "s", dy), self.view(dy), self.grid.neighbour("core", 1))

    def start(self):
        for step in (1, -1):
            self.messages.send(
                (self.name, "y", step), self.view(0), self.grid.neighbour("y", step)
            )
        self.share(0)

    def e1(self):
        for step in (1, -1):
            self.messages.got((self.name, "y", step))
            self.messages.send(
                (self.name, "yh", step),
                self.view(-step, 0 if step == 1 else 1),
                self.grid.neighbour("y", step),
            )
            self.share(-step)

    def e3(self):
        for step in (1, -1):
            self.messages.got((self.name, "yh", step))
        self.share(2)

    def e6(self):
        for dy in (0, 1, -1, 2):
            self.messages.got((self.name, "s", dy))


MESSAGES = 4 * 20 + 4 * 8


def gather_kernel(
    row_ranks, column_ranks, row_left, row_right, column_left, column_right,
    left_out, right_out,
    col_v, col_u, row_v, row_u, core, right, send_sem, recv_sem, local_sem, out_sem,
):
    grid = Grid()
    panels = row_left.shape[0]
    loads = []
    for tile in range(2):
        for source, target in ((column_right, col_v), (column_left, col_u)):
            loads.append((source.at[:, tile], target.at[tile, :, grid.z, grid.x]))
        for source, target in ((row_right, row_v), (row_left, row_u)):
            loads.append((source.at[:, tile], target.at[tile, :, grid.c]))
    loads = [
        pltpu.make_async_copy(source, target, local_sem.at[n])
        for n, (source, target) in enumerate(loads)
    ]
    for load in loads:
        load.start()
    barrier = pltpu.get_barrier_semaphore()
    for axis, step in (("x", 1), ("x", -1), ("z", 1), ("z", -1), ("y", 1), ("y", -1), ("core", 1)):
        pl.semaphore_signal(
            barrier, inc=1, device_id=grid.neighbour(axis, step), device_id_type=MESH
        )
    pl.semaphore_wait(barrier, 7)
    for load in loads:
        load.wait()

    messages = Messages(send_sem, recv_sem)
    v = [
        ColumnStream("v0", grid, messages, col_v.at[0], "x", "z"),
        ColumnStream("v1", grid, messages, col_v.at[1], "z", "x"),
    ]
    u = [
        ColumnStream("u0", grid, messages, col_u.at[0], "x", "z"),
        ColumnStream("u1", grid, messages, col_u.at[1], "z", "x"),
    ]
    rv = [RowStream(f"rv{tile}", grid, messages, row_v.at[tile]) for tile in range(2)]
    ru = [RowStream(f"ru{tile}", grid, messages, row_u.at[tile]) for tile in range(2)]

    def all_of(streams, *names):
        for name in names:
            for stream in streams:
                getattr(stream, name)()

    def cores(col, row):
        rank_c = lax.broadcasted_iota(jnp.int32, core.shape[3:], 0)
        rank_r = lax.broadcasted_iota(jnp.int32, core.shape[3:], 1)

        def one(panel, carry):
            rows, width = SIDE * SIDE * col_v.shape[4], col_v.shape[5]
            value = lax.dot_general(
                col_v[col, panel].reshape(rows, width),
                row_v[row, panel].reshape(rows, width),
                (((0,), (0,)), ((), ())),
                preferred_element_type=jnp.float32,
            )
            keep = (rank_c < column_ranks[panel, col]) & (
                rank_r < row_ranks[panel, grid.r * 2 + row]
            )
            core[col, row, panel] = jnp.where(keep, value, 0.0).astype(core.dtype)
            return carry

        lax.fori_loop(0, panels, one, 0)

    stores = []

    def rights(col, step):
        depth, width = SIDE * col_u.shape[4], col_u.shape[5]
        place = grid.shifted("z" if col == 0 else "x", step)

        def one(turn, carry):
            panel, row = turn // 2, turn % 2
            if col == 0:
                factor = col_u[0, panel, place]
            else:
                factor = col_u[1, panel, :, place]
            value = jnp.dot(
                factor.reshape(depth, width),
                core[col, row, panel],
                preferred_element_type=jnp.float32,
            )
            value = value.astype(right.dtype).reshape(factor.shape)
            if col == 0:
                right[row, 0, panel, place] = value
            else:
                right[row, 1, panel, :, place] = value
            return carry

        lax.fori_loop(0, 2 * panels, one, 0)
        if col == 0:
            source, target = right.at[:, 0, :, place], right_out.at[:, 0, :, place]
        else:
            source, target = right.at[:, 1, :, :, place], right_out.at[:, 1, :, :, place]
        store = pltpu.make_async_copy(source, target, out_sem.at[len(stores)])
        store.start()
        stores.append(store)

    all_of(v, "start_a", "start_b")
    all_of(rv, "start")
    all_of(v, "e1")
    all_of(rv, "e1")
    all_of(v, "e2", "e3")
    all_of(u, "start_a", "start_b")
    all_of(rv, "e3")
    all_of(ru, "start")
    all_of(v, "e4", "e5")
    all_of(u, "e1")
    all_of(ru, "e1")
    all_of(v, "e6")
    all_of(u, "e2")
    all_of(rv, "e6")
    cores(0, 0)
    all_of(u, "e3")
    all_of(ru, "e3")
    cores(0, 1)
    all_of(u, "e4")
    cores(1, 0)
    all_of(u, "e5")
    cores(1, 1)
    all_of(ru, "e6")
    store = pltpu.make_async_copy(row_u, left_out, out_sem.at[0])
    store.start()
    stores.append(store)
    for step in (0, 1, -1):
        for col in range(2):
            rights(col, step)
    for col in range(2):
        u[col].e6()
        rights(col, 2)
    messages.drain()
    for store in stores:
        store.wait()


def gather(row_ranks, column_ranks, row_left, row_right, column_left, column_right):
    panels, rows_here, depth_r, width = row_left.shape
    depth_c = column_left.shape[2]
    bf16 = jnp.bfloat16
    any_space = pl.BlockSpec(memory_space=pl.ANY)
    smem = pl.BlockSpec(memory_space=pltpu.SMEM)
    left_shape = (rows_here, panels, 8, depth_r, width)
    col_shape = (2, panels, SIDE, SIDE, depth_c, width)
    right_shape = (rows_here, 2, panels, SIDE, SIDE, depth_c, width)
    return pl.pallas_call(
        gather_kernel,
        out_shape=(
            jax.ShapeDtypeStruct(left_shape, bf16),
            jax.ShapeDtypeStruct(right_shape, bf16),
        ),
        in_specs=[smem, smem] + [any_space] * 4,
        out_specs=(any_space, any_space),
        scratch_shapes=[
            pltpu.VMEM(col_shape, bf16),
            pltpu.VMEM(col_shape, bf16),
            pltpu.VMEM(left_shape, bf16),
            pltpu.VMEM(left_shape, bf16),
            pltpu.VMEM((2, rows_here, panels, width, width), bf16),
            pltpu.VMEM(right_shape, bf16),
            pltpu.SemaphoreType.DMA((MESSAGES,)),
            pltpu.SemaphoreType.DMA((MESSAGES,)),
            pltpu.SemaphoreType.DMA((8,)),
            pltpu.SemaphoreType.DMA((9,)),
        ],
        compiler_params=pltpu.CompilerParams(
            collective_id=0, has_side_effects=True, vmem_limit_bytes=60 << 20
        ),
        name="gather",
    )(row_ranks, column_ranks, row_left, row_right, column_left, column_right)


def update_kernel(trailing, left, right, out):
    total = trailing[0, 0].astype(jnp.float32)
    for panel in range(left.shape[1]):
        total = total - lax.dot_general(
            left[0, panel],
            right[0, 0, panel],
            (((1,), (1,)), ((), ())),
            preferred_element_type=jnp.float32,
        )
    out[0, 0] = total


def subtract(trailing, left, right):
    rows_here, cols_here, order, _ = trailing.shape
    panels, width = left.shape[1], left.shape[3]
    block = 256
    return pl.pallas_call(
        update_kernel,
        out_shape=jax.ShapeDtypeStruct(trailing.shape, jnp.float32),
        grid=(rows_here, cols_here, order // block),
        in_specs=[
            pl.BlockSpec((1, 1, block, order), lambda i, j, b: (i, j, b, 0)),
            pl.BlockSpec((1, panels, block, width), lambda i, j, b: (i, 0, b, 0)),
            pl.BlockSpec((1, 1, panels, order, width), lambda i, j, b: (i, j, 0, 0, 0)),
        ],
        out_specs=pl.BlockSpec((1, 1, block, order), lambda i, j, b: (i, j, b, 0)),
        compiler_params=pltpu.CompilerParams(vmem_limit_bytes=48 << 20),
        name="subtract",
    )(trailing, left, right)


def on_device(trailing, row_left, row_right, column_left, column_right, row_ranks, column_ranks):
    left, right = gather(row_ranks, column_ranks, row_left, row_right, column_left, column_right)
    rows_here, cols_here, order, _ = trailing.shape
    panels, width = row_left.shape[0], row_left.shape[3]
    left = left.reshape(rows_here, panels, order, width)
    right = right.reshape(rows_here, cols_here, panels, order, width)
    return subtract(trailing, left, right)


def solution(mesh):
    return jax.shard_map(
        on_device,
        mesh=mesh,
        in_specs=(
            P("rows", "cols", None, None),
            P(None, "rows", "cols", None),
            P(None, "rows", "cols", None),
            P(None, "cols", "rows", None),
            P(None, "cols", "rows", None),
            P(),
            P(None, "cols"),
        ),
        out_specs=P("rows", "cols", None, None),
        check_vma=False,
    )
```

time: 280 us -> 103 us (0.37)
  the two profiles are of different devices: /device:TPU:1 before, /device:TPU:0 now
where the time goes in v1:
time: 103 us; the launch traced here: 102 us
  Pallas kernels  98.6 us (96%)
  local copies, waits for them, and re-layouts  3.67 us (4%)
    pallas_call x1, Pallas kernels, gather(): pl.pallas_call(gather_kernel, out_shape=(jax.ShapeDtypeStruct(left_shape,...  73.5 us
    pallas_call x1, Pallas kernels, subtract(): pl.pallas_call(update_kernel, out_shape=jax.ShapeDtypeStruct(trailing.sha...  25.1 us
    unnamed x3, local copies, waits for them, and re-layouts  3.67 us

profile of v1, /device:TPU:0, one launch (start us, length us, event | category | flops | bytes accessed | tf_op | source)
XLA Modules:
  0.0 102.3 jit_solution(3578646212305804406)
XLA Ops:
  0.0 1.3 %copy.8.column_ranks = s32[3,2]{1,0:T(4,128)} copy(s32[3,2]{0,1:T(2,128)} %param.13) | data formatting | bytes 48 | tf_op args[6]
  1.3 73.5 %gather.1 = (bf16[2,3,8,128,384]{4,3,2,1,0:T(8,128)(2,1)}, bf16[2,2,3,4,4,64,384]{6,5,4,3,2,1,0:T(8,128)(2,1)}) custom-call(s32[3,32]{1,0:T(4,128)} %row_ranks.1, s32[3,2]{1,0:T(4,128)} %copy.8.column_ranks, bf16[3,2,128,384]{3,2,1,0:T(8,128)(2,1)} %row_left.1, bf16[3,2,128,384]{3,2,1,0:T(8,128)(2,1)} %row_right.1, bf16[3,2,64,384]{3,2,1,0:T(8,128)(2,1)} %column_left.1, ...), custom_call_target="tpu_custom_call" | custom-call | tf_op jit(solution)/shard_map/gather/pallas_call | solution.py:312
  74.8 0.0 copy-start
  74.8 2.3 %copy-done = bf16[2,3,8,128,384]{4,3,2,1,0:T(8,128)(2,1)S(1)} copy-done((bf16[2,3,8,128,384]{4,3,2,1,0:T(8,128)(2,1)S(1)}, bf16[2,3,8,128,384]{4,3,2,1,0:T(8,128)(2,1)}, u32[]{:S(2)}) %copy-start) | copy-done | bytes 4718616
  77.2 25.1 %subtract.1 = f32[2,2,1024,1024]{3,2,1,0:T(8,128)} custom-call(bf16[2,2,1024,1024]{3,2,1,0:T(8,128)(2,1)} %trailing.1, bf16[2,3,1024,384]{3,2,1,0:T(8,128)(2,1)S(1)} %bitcast.2, bf16[2,2,3,1024,384]{4,3,2,1,0:T(8,128)(2,1)} %bitcast.3), custom_call_target="tpu_custom_call" | custom-call | tf_op jit(solution)/shard_map/subtract/pallas_call | solution.py:355
Async XLA Ops:
  74.8 2.3 %copy-start = (bf16[2,3,8,128,384]{4,3,2,1,0:T(8,128)(2,1)S(1)}, bf16[2,3,8,128,384]{4,3,2,1,0:T(8,128)(2,1)}, u32[]{:S(2)}) copy-start(bf16[2,3,8,128,384]{4,3,2,1,0:T(8,128)(2,1)} %get-tuple-element.7) | copy-start | bytes 14155780

commit v2 on v1

v2 whole, which is shorter than its diff:
```python
import jax
import jax.numpy as jnp
from jax import lax
from jax.experimental import pallas as pl
from jax.experimental.pallas import tpu as pltpu
from jax.sharding import PartitionSpec as P

SIDE = 4
MESH = pl.DeviceIdType.MESH


class Grid:
    def __init__(self):
        self.r = lax.axis_index("rows")
        self.c = lax.axis_index("cols")
        self.z, self.x = self.r // SIDE, self.r % SIDE
        self.y, self.core = self.c // 2, self.c % 2

    def shifted(self, axis, step):
        return (getattr(self, axis) + (step + SIDE)) % SIDE

    def neighbour(self, axis, step):
        if axis == "z":
            return (self.shifted("z", step) * SIDE + self.x, self.c)
        if axis == "x":
            return (self.z * SIDE + self.shifted("x", step), self.c)
        if axis == "y":
            return (self.r, self.shifted("y", step) * 2 + self.core)
        return (self.r, self.y * 2 + (1 - self.core))


class Messages:
    def __init__(self, send_sem, recv_sem):
        self.send_sem, self.recv_sem = send_sem, recv_sem
        self.sent = {}

    def send(self, key, view, target):
        index = len(self.sent)
        copy = pltpu.make_async_remote_copy(
            src_ref=view,
            dst_ref=view,
            send_sem=self.send_sem.at[index],
            recv_sem=self.recv_sem.at[index],
            device_id=target,
            device_id_type=MESH,
        )
        copy.start()
        self.sent[key] = copy

    def got(self, key):
        self.sent[key].wait_recv()

    def drain(self):
        for copy in self.sent.values():
            copy.wait_send()


class ColumnStream:
    def __init__(self, name, grid, messages, buf, first, second):
        self.name, self.grid, self.messages, self.buf = name, grid, messages, buf
        self.a, self.b = first, second

    def view(self, da, db, half=None):
        place = {self.a: self.grid.shifted(self.a, da), self.b: self.grid.shifted(self.b, db)}
        if half is None:
            return self.buf.at[:, place["z"], place["x"]]
        part = self.buf.shape[3] // 2
        return self.buf.at[:, place["z"], place["x"], pl.ds(half * part, part)]

    def send(self, kind, da, db, axis, step, half=None):
        self.messages.send(
            (self.name, kind, da, step), self.view(da, db, half), self.grid.neighbour(axis, step)
        )

    def got(self, kind, da, step):
        self.messages.got((self.name, kind, da, step))

    def start_a(self):
        for step in (1, -1):
            self.send("a", 0, 0, self.a, step)

    def start_b(self):
        for step in (1, -1):
            self.send("b", 0, 0, self.b, step)

    def e1(self):
        for step in (1, -1):
            self.got("a", 0, step)
            self.messages.send(
                (self.name, "ah", 0, step),
                self.view(-step, 0, 0 if step == 1 else 1),
                self.grid.neighbour(self.a, step),
            )
            for out in (1, -1):
                self.send("b", -step, 0, self.b, out)

    def relay(self, da):
        for step in (1, -1):
            self.got("b", da, step)
            self.send("bh", da, -step, self.b, step, 0 if step == 1 else 1)

    def e2(self):
        self.relay(0)

    def e3(self):
        for step in (1, -1):
            self.got("ah", 0, step)
        for out in (1, -1):
            self.send("b", 2, 0, self.b, out)

    def e4(self):
        self.relay(1)
        self.relay(-1)

    def e5(self):
        self.relay(2)

    def e6(self):
        for da in (0, 1, -1, 2):
            for step in (1, -1):
                self.got("bh", da, step)


class RowStream:
    def __init__(self, name, grid, messages, buf):
        self.name, self.grid, self.messages, self.buf = name, grid, messages, buf

    def view(self, dy, half=None):
        place = self.grid.shifted("y", dy)
        if half is None:
            return self.buf.at[:, place, self.grid.core]
        part = self.buf.shape[3] // 2
        return self.buf.at[:, place, self.grid.core, pl.ds(half * part, part)]

    def share(self, dy):
        self.messages.send((self.name, "s", dy), self.view(dy), self.grid.neighbour("core", 1))

    def start(self):
        for step in (1, -1):
            self.messages.send(
                (self.name, "y", step), self.view(0), self.grid.neighbour("y", step)
            )
        self.share(0)

    def e1(self):
        for step in (1, -1):
            self.messages.got((self.name, "y", step))
            self.messages.send(
                (self.name, "yh", step),
                self.view(-step, 0 if step == 1 else 1),
                self.grid.neighbour("y", step),
            )
            self.share(-step)

    def e3(self):
        for step in (1, -1):
            self.messages.got((self.name, "yh", step))
        self.share(2)

    def e6(self):
        for dy in (0, 1, -1, 2):
            self.messages.got((self.name, "s", dy))


MESSAGES = 4 * 20 + 2 * 8


def gather_kernel(
    row_ranks, column_ranks, trailing, row_left, row_right, column_left, column_right,
    out,
    col_v, col_u, row_v, row_u, total, core, right, dense, send_sem, recv_sem, local_sem,
):
    grid = Grid()
    panels, tiles, depth_r, width = row_left.shape
    depth_c = column_left.shape[2]
    chunk = SIDE * depth_c
    loads = []
    for tile in range(2):
        for source, target in ((column_right, col_v), (column_left, col_u)):
            loads.append((source.at[:, tile], target.at[tile, :, grid.z, grid.x]))
        lanes = pl.ds(tile * width, width)
        loads.append((row_right.at[:, tile], row_v.at[:, grid.y, grid.core, :, lanes]))
    for panel in range(panels):
        lanes = pl.ds(panel * width, width)
        loads.append((row_left.at[panel], row_u.at[:, grid.y, grid.core, :, lanes]))
    loads.append((trailing, dense))
    loads = [
        pltpu.make_async_copy(source, target, local_sem.at[n])
        for n, (source, target) in enumerate(loads)
    ]
    for load in loads:
        load.start()
    barrier = pltpu.get_barrier_semaphore()
    for axis, step in (("x", 1), ("x", -1), ("z", 1), ("z", -1), ("y", 1), ("y", -1), ("core", 1)):
        pl.semaphore_signal(
            barrier, inc=1, device_id=grid.neighbour(axis, step), device_id_type=MESH
        )
    pl.semaphore_wait(barrier, 7)
    for load in loads[:-1]:
        load.wait()

    messages = Messages(send_sem, recv_sem)
    v = [
        ColumnStream("v0", grid, messages, col_v.at[0], "x", "z"),
        ColumnStream("v1", grid, messages, col_v.at[1], "z", "x"),
    ]
    u = [
        ColumnStream("u0", grid, messages, col_u.at[0], "x", "z"),
        ColumnStream("u1", grid, messages, col_u.at[1], "z", "x"),
    ]
    rv = [RowStream("rv", grid, messages, row_v)]
    ru = [RowStream("ru", grid, messages, row_u)]

    def all_of(streams, *names):
        for name in names:
            for stream in streams:
                getattr(stream, name)()

    def widen():
        def one(turn, carry):
            rows = pl.ds(pl.multiple_of((turn % 4) * chunk, chunk), chunk)
            out[turn // 4, 1, rows] = dense[turn // 4, 1, rows].astype(jnp.float32)
            return carry

        lax.fori_loop(0, 4 * tiles, one, 0)

    def cores(col, step, first=False, last=False):
        place = grid.shifted("z" if col == 0 else "x", step)

        def one(panel, carry):
            if col == 0:
                left_side, right_side = col_v[0, panel, place], row_v[panel, place]
            else:
                start = pl.multiple_of((place % 2) * depth_c, depth_c)
                left_side = col_v[1, panel, :, place]
                right_side = row_v[panel, :, place // 2, pl.ds(start, depth_c)]
            value = lax.dot_general(
                left_side.reshape(chunk, width),
                right_side.reshape(chunk, tiles * width),
                (((0,), (0,)), ((), ())),
                preferred_element_type=jnp.float32,
            )
            if not first:
                value = value + total[col, panel]
            if last:
                shape = value.shape
                lane = lax.broadcasted_iota(jnp.int32, shape, 1)
                limit = jnp.where(
                    lane < width,
                    row_ranks[panel, grid.r * 2],
                    row_ranks[panel, grid.r * 2 + 1] + width,
                )
                keep = (lane < limit) & (
                    lax.broadcasted_iota(jnp.int32, shape, 0) < column_ranks[col, panel]
                )
                core[col, panel] = jnp.where(keep, value, 0.0).astype(core.dtype)
            else:
                total[col, panel] = value
            return carry

        lax.fori_loop(0, panels, one, 0)

    def updates(col, step):
        place = grid.shifted("z" if col == 0 else "x", step)
        half = place % 2
        for panel in range(panels):
            factor = col_u[0, panel, place] if col == 0 else col_u[1, panel, :, place]
            value = jnp.dot(
                factor.reshape(chunk, width), core[col, panel], preferred_element_type=jnp.float32
            ).astype(right.dtype)
            for tile in range(tiles):
                lanes = pl.ds(panel * width, width)
                piece = value[:, tile * width : (tile + 1) * width]
                if col == 0:
                    right[tile, :, lanes] = piece
                    continue
                for group in range(SIDE):
                    side = half if group < 2 else 1 - half
                    start = pl.multiple_of((group % 2) * 2 * depth_c + side * depth_c, depth_c)
                    right[tile, pl.ds(start, depth_c), lanes] = piece[
                        group * depth_c : (group + 1) * depth_c
                    ]

        def one(turn, carry):
            tile, part = turn // 2, turn % 2
            rows = 2 * chunk
            value = lax.dot_general(
                row_u[tile, pl.ds(part * 2, 2)].reshape(rows, panels * width),
                right[tile],
                (((1,), (1,)), ((), ())),
                preferred_element_type=jnp.float32,
            )
            here = pl.ds(pl.multiple_of(part * rows, rows), rows)
            if col == 0:
                lanes = pl.ds(pl.multiple_of(place * chunk, chunk), chunk)
                out[tile, 0, here, lanes] = dense[tile, 0, here, lanes].astype(jnp.float32) - value
                return carry
            span = 2 * depth_c
            mine = lax.broadcasted_iota(jnp.int32, (rows, span), 1) // depth_c == half
            for group in range(SIDE):
                piece = value[:, (group % 2) * span : (group % 2 + 1) * span]
                if group >= 2:
                    piece = pltpu.roll(piece, depth_c, 1)
                lanes = pl.ds(pl.multiple_of((group * 2 + place // 2) * span, span), span)
                out[tile, 1, here, lanes] = out[tile, 1, here, lanes] - jnp.where(mine, piece, 0.0)
            return carry

        lax.fori_loop(0, 2 * tiles, one, 0)

    all_of(v, "start_a", "start_b")
    all_of(rv, "start")
    all_of(v, "e1")
    loads[-1].wait()
    widen()
    all_of(v, "e2")
    all_of(rv, "e1")
    all_of(v, "e3")
    all_of(u, "start_a", "start_b")
    all_of(rv, "e3")
    all_of(ru, "start")
    all_of(v, "e4", "e5")
    all_of(u, "e1")
    all_of(rv, "e6")
    for col in range(2):
        cores(col, 0, first=True)
    all_of(u, "e2")
    for col in range(2):
        cores(col, 1)
    all_of(ru, "e1")
    for col in range(2):
        cores(col, -1)
    all_of(u, "e3")
    all_of(v, "e6")
    for col in range(2):
        cores(col, 2, last=True)
    all_of(u, "e4")
    all_of(ru, "e3", "e6")
    updates(0, 0)
    all_of(u, "e5")
    updates(1, 0)
    for step in (1, -1):
        for col in range(2):
            updates(col, step)
    for col in range(2):
        u[col].e6()
        updates(col, 2)
    messages.drain()


def on_device(trailing, row_left, row_right, column_left, column_right, row_ranks, column_ranks):
    panels, tiles, depth_r, width = row_left.shape
    depth_c = column_left.shape[2]
    order = trailing.shape[3]
    bf16 = jnp.bfloat16
    any_space = pl.BlockSpec(memory_space=pl.ANY)
    smem = pl.BlockSpec(memory_space=pltpu.SMEM)
    col_shape = (2, panels, SIDE, SIDE, depth_c, width)
    return pl.pallas_call(
        gather_kernel,
        out_shape=pltpu.VMEM(trailing.shape, jnp.float32),
        in_specs=[smem, smem] + [any_space] * 5,
        out_specs=pl.BlockSpec(memory_space=pltpu.VMEM),
        scratch_shapes=[
            pltpu.VMEM(col_shape, bf16),
            pltpu.VMEM(col_shape, bf16),
            pltpu.VMEM((panels, SIDE, 2, depth_r, tiles * width), bf16),
            pltpu.VMEM((tiles, SIDE, 2, depth_r, panels * width), bf16),
            pltpu.VMEM((2, panels, width, tiles * width), jnp.float32),
            pltpu.VMEM((2, panels, width, tiles * width), bf16),
            pltpu.VMEM((tiles, SIDE * depth_c, panels * width), bf16),
            pltpu.VMEM(trailing.shape, bf16),
            pltpu.SemaphoreType.DMA((MESSAGES,)),
            pltpu.SemaphoreType.DMA((MESSAGES,)),
            pltpu.SemaphoreType.DMA((10,)),
        ],
        compiler_params=pltpu.CompilerParams(
            collective_id=0, has_side_effects=True, vmem_limit_bytes=LIMIT
        ),
        name="gather_update",
    )(row_ranks, column_ranks.T, trailing, row_left, row_right, column_left, column_right)


LIMIT = 46 << 20


def solution(mesh):
    return jax.shard_map(
        on_device,
        mesh=mesh,
        in_specs=(
            P("rows", "cols", None, None),
            P(None, "rows", "cols", None),
            P(None, "rows", "cols", None),
            P(None, "cols", "rows", None),
            P(None, "cols", "rows", None),
            P(),
            P(None, "cols"),
        ),
        out_specs=P("rows", "cols", None, None),
        check_vma=False,
    )
```

time: 103 us -> 88.2 us (0.86)
  the two profiles are of different devices: /device:TPU:0 before, /device:TPU:1 now
where the time goes in v2:
time: 88.2 us; the launch traced here: 88 us
  Pallas kernels  81.9 us (93%)
  local copies, waits for them, and re-layouts  6.16 us (7%)
    pallas_call x1, Pallas kernels, on_device(): pl.pallas_call(gather_kernel, out_shape=pltpu.VMEM(trailing.shape, jnp.fl...  81.9 us
    unnamed x1, local copies, waits for them, and re-layouts  6.16 us

profile of v2, /device:TPU:1, one launch (start us, length us, event | category | flops | bytes accessed | tf_op | source)
XLA Modules:
  0.0 88.0 jit_solution(16214934824299692583)
XLA Ops:
  0.0 81.9 %gather_update.1 = f32[2,2,1024,1024]{3,2,1,0:T(8,128)S(1)} custom-call(s32[3,32]{1,0:T(4,128)} %row_ranks.1, s32[2,3]{1,0:T(2,128)} %bitcast.1, bf16[2,2,1024,1024]{3,2,1,0:T(8,128)(2,1)} %trailing.1, bf16[3,2,128,384]{3,2,1,0:T(8,128)(2,1)} %row_left.1, bf16[3,2,128,384]{3,2,1,0:T(8,128)(2,1)} %row_right.1, bf16[3,2,64,384]{3,2,1,0:T(8,128)(2,1)} %column_left.1, ...), custom_call_target="tpu_custom_call" | custom-call | tf_op jit(solution)/shard_map/gather_update/pallas_call | solution.py:358
  81.9 6.2 %copy.9 = f32[2,2,1024,1024]{3,2,1,0:T(8,128)} copy(f32[2,2,1024,1024]{3,2,1,0:T(8,128)S(1)} %gather_update.1) | data formatting | bytes 33554432

commit v3 on v2

--- a/solution.py
+++ b/solution.py
@@ -336,8 +336,8 @@
     all_of(u, "e4")
     all_of(ru, "e3", "e6")
     updates(0, 0)
+    updates(1, 0)
     all_of(u, "e5")
-    updates(1, 0)
     for step in (1, -1):
         for col in range(2):
             updates(col, step)

time: 88.2 us -> 88.1 us (level)
  no operation moved by 1% of the time
where the time goes in v3:
time: 88.1 us; the launch traced here: 88 us
  Pallas kernels  81.8 us (93%)
  local copies, waits for them, and re-layouts  6.16 us (7%)
    pallas_call x1, Pallas kernels, on_device(): pl.pallas_call(gather_kernel, out_shape=pltpu.VMEM(trailing.shape, jnp.fl...  81.8 us
    unnamed x1, local copies, waits for them, and re-layouts  6.16 us

profile of v3, /device:TPU:1, one launch (start us, length us, event | category | flops | bytes accessed | tf_op | source)
XLA Modules:
  0.0 88.0 jit_solution(17968346682202552961)
XLA Ops:
  0.0 81.8 %gather_update.1 = f32[2,2,1024,1024]{3,2,1,0:T(8,128)S(1)} custom-call(s32[3,32]{1,0:T(4,128)} %row_ranks.1, s32[2,3]{1,0:T(2,128)} %bitcast.1, bf16[2,2,1024,1024]{3,2,1,0:T(8,128)(2,1)} %trailing.1, bf16[3,2,128,384]{3,2,1,0:T(8,128)(2,1)} %row_left.1, bf16[3,2,128,384]{3,2,1,0:T(8,128)(2,1)} %row_right.1, bf16[3,2,64,384]{3,2,1,0:T(8,128)(2,1)} %column_left.1, ...), custom_call_target="tpu_custom_call" | custom-call | tf_op jit(solution)/shard_map/gather_update/pallas_call | solution.py:358
  81.8 6.2 %copy.9 = f32[2,2,1024,1024]{3,2,1,0:T(8,128)} copy(f32[2,2,1024,1024]{3,2,1,0:T(8,128)S(1)} %gather_update.1) | data formatting | bytes 33554432
